TPU v7x, 512 devices: a whole 4x8x8 slice. The times are simulated.
512 devices in a mesh: dp: 8 (over z_lo, core), seq: 64 (over z_hi, y, x).
Axes of the slice: x: 4, y: 8, z: 8 (z_hi: 2, z_lo: 4; z = z_hi * 4 + z_lo), core: 2. Of those that a mesh axis runs over, the one named last changes fastest.
Arguments:
- value_branch: bfloat16 [512, 65536], P(None, ('dp', 'seq')), parts along dimension 1, may hold values from -6 to 6
- first_gate: bfloat16 [512, 65536], P(None, ('dp', 'seq')), parts along dimension 1, may hold values from -6 to 6
- second_gate: bfloat16 [512, 65536], P(None, ('dp', 'seq')), parts along dimension 1, may hold values from -6 to 6
- out_cotangent: bfloat16 [512, 65536], P(None, ('dp', 'seq')), parts along dimension 1, may hold values from -6 to 6
- pos_weight: float32 [64, 33], replicated, may hold values from -4 to 4
- pos_bias: float32 [64], replicated, may hold values from -3.140625 to 3.140625
- mid_weight: float32 [64, 64], replicated, may hold values from -0.75 to 0.75
- mid_bias: float32 [64], replicated, may hold values from -3.140625 to 3.140625
- out_weight: float32 [1024, 64], replicated, may hold values from -0.0234375 to 0.0234375
- decay_rates: float32 [1024], replicated, may hold values from 3.07 to 15.35
Outputs:
- value_grad: bfloat16 [512, 65536], P(None, ('dp', 'seq')), parts along dimension 1
- first_gate_grad: bfloat16 [512, 65536], P(None, ('dp', 'seq')), parts along dimension 1
- second_gate_grad: bfloat16 [512, 65536], P(None, ('dp', 'seq')), parts along dimension 1
- pos_weight_grad: float32 [512, 33], P('dp'), parts along dimension 0
- pos_bias_grad: float32 [512], P('dp'), parts along dimension 0
- mid_weight_grad: float32 [512, 64], P('dp'), parts along dimension 0
- mid_bias_grad: float32 [512], P('dp'), parts along dimension 0
- out_weight_grad: float32 [1024, 512], P('seq', 'dp'), parts along dimension 1
There are 8 independent parts, one for each index of `dp`. A program takes and returns all parts, laid end to end along the dimension named above; an argument that names none is the same for every part. Nothing has to cross between parts.
All inputs are finite; a program needn't handle non-finite values.
Results may differ from a plain program's by a relative error of at most 0.017.
Values may be sent and summed in bfloat16 or wider, within the bound.
No kernel may reach another device: no remote copies, remote signals or barrier semaphores. Data moves between devices by JAX's collectives and lax.ppermute only.
A program may use at most 64 MiB of HBM per device.

v0:
```python
import math
import jax
import jax.numpy as jnp
from jax import lax
from jax.sharding import PartitionSpec as P

RADIX = 128


def make_tables(freq_rows, radix):
    length_all = freq_rows * radix
    freq_index = jnp.arange(freq_rows, dtype=jnp.int32)
    half_index = jnp.arange(freq_rows // 2, dtype=jnp.int32)
    inner_index = jnp.arange(radix, dtype=jnp.int32)
    angle_one = (freq_index[:, None] * half_index[None, :] % freq_rows).astype(jnp.float32) * (
        2.0 * math.pi / freq_rows
    )
    angle_two = (inner_index[:, None] * inner_index[None, :] % radix).astype(jnp.float32) * (
        2.0 * math.pi / radix
    )
    angle_twid = (freq_index[:, None] * inner_index[None, :] % length_all).astype(jnp.float32) * (
        2.0 * math.pi / length_all
    )
    cos_one = jnp.cos(angle_one).astype(jnp.bfloat16)
    sin_one = jnp.sin(angle_one).astype(jnp.bfloat16)
    cos_two = jnp.cos(angle_two).astype(jnp.bfloat16)
    sin_two = jnp.sin(angle_two).astype(jnp.bfloat16)
    left_table = jnp.concatenate([cos_one, -sin_one], axis=0)
    right_fwd = jnp.concatenate(
        [jnp.concatenate([cos_two, -sin_two], axis=1), jnp.concatenate([sin_two, cos_two], axis=1)],
        axis=0,
    )
    right_inv = jnp.concatenate(
        [jnp.concatenate([cos_two, sin_two], axis=1), jnp.concatenate([-sin_two, cos_two], axis=1)],
        axis=0,
    )
    return (left_table, right_fwd, right_inv, jnp.cos(angle_twid), jnp.sin(angle_twid))


def forward_spectrum(signal, tables, freq_rows, radix):
    left_table, right_fwd, right_inv, twid_cos, twid_sin = tables
    count = signal.shape[0]
    shaped = signal.reshape(count, freq_rows // 2, radix)
    stacked = jnp.einsum("kn,rnm->rkm", left_table, shaped, preferred_element_type=jnp.float32)
    real_a = stacked[:, :freq_rows]
    imag_a = stacked[:, freq_rows:]
    real_b = (real_a * twid_cos + imag_a * twid_sin).astype(jnp.bfloat16)
    imag_b = (imag_a * twid_cos - real_a * twid_sin).astype(jnp.bfloat16)
    joined = jnp.concatenate([real_b, imag_b], axis=2)
    spectrum = jnp.einsum("rkn,nm->rkm", joined, right_fwd, preferred_element_type=jnp.float32)
    return (spectrum[:, :, :radix], spectrum[:, :, radix:])


def inverse_signal(product, tables, freq_rows, radix):
    left_table, right_fwd, right_inv, twid_cos, twid_sin = tables
    real_p, imag_p = product
    joined = jnp.concatenate([real_p, imag_p], axis=2)
    section_q = jnp.einsum("rkn,nm->rkm", joined, right_inv, preferred_element_type=jnp.float32)
    real_q = section_q[:, :, :radix]
    imag_q = section_q[:, :, radix:]
    real_r = (real_q * twid_cos - imag_q * twid_sin).astype(jnp.bfloat16)
    imag_r = (imag_q * twid_cos + real_q * twid_sin).astype(jnp.bfloat16)
    rows_both = jnp.concatenate([real_r, imag_r], axis=1)
    output = jnp.einsum("kn,rkm->rnm", left_table, rows_both, preferred_element_type=jnp.float32)
    count = real_p.shape[0]
    return (output * (1.0 / (freq_rows * radix))).reshape(count, freq_rows // 2 * radix)


def spectral_product(left, right, conj_left, conj_right):
    sign_left = -1.0 if conj_left else 1.0
    sign_right = -1.0 if conj_right else 1.0
    real_part = left[0] * right[0] - sign_left * sign_right * left[1] * right[1]
    imag_part = sign_left * left[1] * right[0] + sign_right * left[0] * right[1]
    return (real_part.astype(jnp.bfloat16), imag_part.astype(jnp.bfloat16))


def positional_features(positions, seq_len, bands):
    band_index = jnp.arange(1, bands + 1, dtype=jnp.int32)
    angles = (band_index[:, None] * positions[None, :] % seq_len).astype(jnp.float32) * (
        2.0 * math.pi / seq_len
    )
    ramp = positions.astype(jnp.float32)[None, :] / seq_len
    return jnp.concatenate([ramp, jnp.cos(angles), jnp.sin(angles)], axis=0)


def filter_network(positions, seq_len, pos_weight, pos_bias, mid_weight, mid_bias):
    bands = (pos_weight.shape[1] - 1) // 2
    features = positional_features(positions, seq_len, bands)
    pre_one = jnp.dot(pos_weight, features, precision=lax.Precision.HIGHEST) + pos_bias[:, None]
    act_one = jnp.sin(pre_one)
    pre_two = jnp.dot(mid_weight, act_one, precision=lax.Precision.HIGHEST) + mid_bias[:, None]
    act_two = jnp.sin(pre_two)
    return (features, pre_one, act_one, pre_two, act_two)


def modulation(rates, positions, seq_len):
    return jnp.exp(-rates[:, None] * positions.astype(jnp.float32)[None, :] / seq_len)


def contract_last(left, right):
    return lax.dot_general(left, right, (((1,), (1,)), ((), ())), precision=lax.Precision.HIGHEST)


def network_backward(act_grad, features, pre_one, act_one, pre_two, mid_weight):
    pre_two_grad = act_grad * jnp.cos(pre_two)
    mid_weight_part = contract_last(pre_two_grad, act_one)
    mid_bias_part = jnp.sum(pre_two_grad, axis=1)
    pre_one_grad = jnp.dot(mid_weight.T, pre_two_grad, precision=lax.Precision.HIGHEST) * jnp.cos(
        pre_one
    )
    pos_weight_part = contract_last(pre_one_grad, features)
    pos_bias_part = jnp.sum(pre_one_grad, axis=1)
    return (pos_weight_part, pos_bias_part, mid_weight_part, mid_bias_part)


def on_device(
    value_branch,
    first_gate,
    second_gate,
    out_cotangent,
    pos_weight,
    pos_bias,
    mid_weight,
    mid_bias,
    out_weight,
    decay_rates,
):
    model_width, tok_dev = value_branch.shape
    devices = lax.axis_size("seq")
    seq_len = tok_dev * devices
    channels = model_width // devices
    my_rank = lax.axis_index("seq")
    freq_rows = 2 * seq_len // RADIX
    tables = make_tables(freq_rows, RADIX)
    all_positions = jnp.arange(seq_len, dtype=jnp.int32)
    own_rates = lax.dynamic_slice_in_dim(decay_rates, my_rank * 2 * channels, 2 * channels)
    window_own = modulation(own_rates, all_positions, seq_len)
    value_ch, first_ch = (
        lax.all_to_all(value_branch, "seq", split_axis=0, concat_axis=1, tiled=True),
        lax.all_to_all(first_gate, "seq", split_axis=0, concat_axis=1, tiled=True),
    )
    local_positions = my_rank * tok_dev + jnp.arange(tok_dev, dtype=jnp.int32)
    features, pre_one, act_one, pre_two, act_two = filter_network(
        local_positions, seq_len, pos_weight, pos_bias, mid_weight, mid_bias
    )
    window_local = modulation(decay_rates, local_positions, seq_len)
    local_filters = (
        jnp.dot(out_weight, act_two, precision=lax.Precision.HIGHEST) * window_local
    ).astype(jnp.bfloat16)
    filt_ch = lax.all_to_all(local_filters, "seq", split_axis=0, concat_axis=1, tiled=True)
    filt_real, filt_imag = forward_spectrum(filt_ch, tables, freq_rows, RADIX)
    filt_real = filt_real.reshape(channels, 2, freq_rows, RADIX)
    filt_imag = filt_imag.reshape(channels, 2, freq_rows, RADIX)
    spec_one = (filt_real[:, 0], filt_imag[:, 0])
    spec_two = (filt_real[:, 1], filt_imag[:, 1])
    spec_val = forward_spectrum(value_ch, tables, freq_rows, RADIX)
    conv_one = inverse_signal(
        spectral_product(spec_one, spec_val, False, False), tables, freq_rows, RADIX
    )
    gated = (first_ch.astype(jnp.float32) * conv_one).astype(jnp.bfloat16)
    spec_gated = forward_spectrum(gated, tables, freq_rows, RADIX)
    conv_two = inverse_signal(
        spectral_product(spec_two, spec_gated, False, False), tables, freq_rows, RADIX
    )
    second_ch, cot_ch = (
        lax.all_to_all(second_gate, "seq", split_axis=0, concat_axis=1, tiled=True),
        lax.all_to_all(out_cotangent, "seq", split_axis=0, concat_axis=1, tiled=True),
    )
    cot_wide = cot_ch.astype(jnp.float32)
    second_grad_ch = (cot_wide * conv_two).astype(jnp.bfloat16)
    second_out = lax.all_to_all(second_grad_ch, "seq", split_axis=1, concat_axis=0, tiled=True)
    grad_two = (cot_wide * second_ch.astype(jnp.float32)).astype(jnp.bfloat16)
    spec_gtwo = forward_spectrum(grad_two, tables, freq_rows, RADIX)
    gated_grad = inverse_signal(
        spectral_product(spec_two, spec_gtwo, True, False), tables, freq_rows, RADIX
    )
    filt_grad_two = inverse_signal(
        spectral_product(spec_gtwo, spec_gated, False, True), tables, freq_rows, RADIX
    )
    first_grad_ch = (gated_grad * conv_one).astype(jnp.bfloat16)
    grad_one = (gated_grad * first_ch.astype(jnp.float32)).astype(jnp.bfloat16)
    spec_gone = forward_spectrum(grad_one, tables, freq_rows, RADIX)
    value_grad_ch = inverse_signal(
        spectral_product(spec_one, spec_gone, True, False), tables, freq_rows, RADIX
    ).astype(jnp.bfloat16)
    filt_grad_one = inverse_signal(
        spectral_product(spec_gone, spec_val, False, True), tables, freq_rows, RADIX
    )
    value_out, first_out = (
        lax.all_to_all(value_grad_ch, "seq", split_axis=1, concat_axis=0, tiled=True),
        lax.all_to_all(first_grad_ch, "seq", split_axis=1, concat_axis=0, tiled=True),
    )
    filt_grads = jnp.stack([filt_grad_one, filt_grad_two], axis=1).reshape(2 * channels, seq_len)
    filter_grad_ch = filt_grads * window_own / seq_len
    filter_grad_seq = lax.all_to_all(
        filter_grad_ch.astype(jnp.bfloat16), "seq", split_axis=1, concat_axis=0, tiled=True
    ).astype(filter_grad_ch.dtype)
    out_weight_grad = lax.psum_scatter(
        contract_last(filter_grad_seq, act_two), "seq", scatter_dimension=0, tiled=True
    )
    act_grad = jnp.dot(out_weight.T, filter_grad_seq, precision=lax.Precision.HIGHEST)
    partials = network_backward(act_grad, features, pre_one, act_one, pre_two, mid_weight)
    pos_weight_grad, pos_bias_grad, mid_weight_grad, mid_bias_grad = lax.psum(
        (partials[0], partials[1], partials[2], partials[3]), "seq"
    )
    return (
        value_out,
        first_out,
        second_out,
        pos_weight_grad,
        pos_bias_grad,
        mid_weight_grad,
        mid_bias_grad,
        out_weight_grad,
    )


def solution(mesh):
    in_specs = (
        P(None, ("dp", "seq")),
        P(None, ("dp", "seq")),
        P(None, ("dp", "seq")),
        P(None, ("dp", "seq")),
        P(),
        P(),
        P(),
        P(),
        P(),
        P(),
    )
    out_specs = (
        P(None, ("dp", "seq")),
        P(None, ("dp", "seq")),
        P(None, ("dp", "seq")),
        P("dp", None),
        P("dp"),
        P("dp", None),
        P("dp"),
        P("seq", "dp"),
    )
    return jax.shard_map(
        on_device, mesh=mesh, in_specs=in_specs, out_specs=out_specs, check_vma=False
    )
```

profile of v0, /device:TPU:64, one launch (start us, length us, event | category | flops | bytes accessed | tf_op | source)
XLA Modules:
  0.0 657.4 jit_solution(1359038051351091509)
XLA Ops:
  7.2 18.3 %all-to-all-start.1 = ((bf16[64,8,128]{2,1,0:T(8,128)(2,1)}), bf16[64,8,128]{2,1,0:T(8,128)(2,1)S(1)}, u32[]{:S(2)}, u32[]{:S(2)}) async-start(bf16[64,8,128]{2,1,0:T(8,128)(2,1)} %bitcast.181), calls=%async_computation.1 | async-start | bytes 262144 | tf_op jit(solution)/shard_map/all_to_all | solution.py:167
  26.4 1.6 fusion.148
  28.7 1.6 fusion.149
  30.3 10.2 %all-to-all-done.1 = bf16[64,8,128]{2,1,0:T(8,128)(2,1)S(1)} async-done(((bf16[64,8,128]{2,1,0:T(8,128)(2,1)}), bf16[64,8,128]{2,1,0:T(8,128)(2,1)S(1)}, u32[]{:S(2)}, u32[]{:S(2)}) %all-to-all-start.1) | async-done | bytes 131104 | tf_op jit(solution)/shard_map/all_to_all | solution.py:167
  40.5 5.0 all-to-all-start.5
  45.7 0.7 neg.17
  46.4 0.6 fusion.1
  47.0 13.6 %all-to-all-done.5 = bf16[64,8,128]{2,1,0:T(8,128)(2,1)S(1)} async-done(((bf16[64,8,128]{2,1,0:T(8,128)(2,1)}), bf16[64,8,128]{2,1,0:T(8,128)(2,1)S(1)}, u32[]{:S(2)}, u32[]{:S(2)}) %all-to-all-start.5) | async-done | bytes 131104 | tf_op jit(solution)/shard_map/all_to_all | solution.py:139
  60.6 4.6 all-to-all-start.2
  65.6 0.8 copy.93
  66.8 13.5 %all-to-all-done.2 = bf16[64,8,128]{2,1,0:T(8,128)(2,1)S(1)} async-done(((bf16[64,8,128]{2,1,0:T(8,128)(2,1)}), bf16[64,8,128]{2,1,0:T(8,128)(2,1)S(1)}, u32[]{:S(2)}, u32[]{:S(2)}) %all-to-all-start.2) | async-done | bytes 131104 | tf_op jit(solution)/shard_map/all_to_all | solution.py:166
  80.3 4.6 all-to-all-start
  86.3 14.5 %all-to-all-done = bf16[64,16,128]{2,1,0:T(8,128)(2,1)S(1)} async-done(((bf16[64,16,128]{2,1,0:T(8,128)(2,1)}), bf16[64,16,128]{2,1,0:T(8,128)(2,1)S(1)}, u32[]{:S(2)}, u32[]{:S(2)}) %all-to-all-start) | async-done | bytes 262176 | tf_op jit(solution)/shard_map/all_to_all | solution.py:150
  100.8 5.6 all-to-all-start.3
  106.4 0.5 convolution_bitcast_fusion
  107.2 0.5 fusion.9
  108.3 0.6 copy-done.1
  109.4 1.0 fusion.4
  110.5 1.3 fusion.17
  111.8 9.3 %all-to-all-done.3 = bf16[64,8,128]{2,1,0:T(8,128)(2,1)} async-done(((bf16[64,8,128]{2,1,0:T(8,128)(2,1)}), bf16[64,8,128]{2,1,0:T(8,128)(2,1)}, u32[]{:S(2)}, u32[]{:S(2)}) %all-to-all-start.3) | async-done | bytes 131104 | tf_op jit(solution)/shard_map/all_to_all | solution.py:140
  121.1 1.4 convolution_bitcast_fusion.1
  122.6 1.2 add_convert_fusion.7
  124.3 0.4 copy-done.10
  124.7 0.9 multiply_convert_fusion.1
  125.6 1.3 convolution_bitcast_fusion.3
  129.5 0.6 subtract_convert_fusion.3
  130.7 0.7 copy.126
  131.4 5.6 all-to-all-start.7
  137.4 0.7 copy.115
  138.1 14.0 %all-to-all-done.7 = bf16[8,64,128]{2,0,1:T(8,128)(2,1)S(1)} async-done(((bf16[8,64,128]{2,0,1:T(8,128)(2,1)}), bf16[8,64,128]{2,0,1:T(8,128)(2,1)S(1)}, u32[]{:S(2)}, u32[]{:S(2)}) %all-to-all-start.7) | async-done | bytes 131104 | tf_op jit(solution)/shard_map/all_to_all | solution.py:171
  152.1 4.6 all-to-all-start.4
  156.7 0.8 dynamic-slice_negate_fusion
  157.5 0.7 copy.121
  158.8 12.9 %all-to-all-done.4 = bf16[8,64,128]{2,0,1:T(8,128)(2,1)S(1)} async-done(((bf16[8,64,128]{2,0,1:T(8,128)(2,1)}), bf16[8,64,128]{2,0,1:T(8,128)(2,1)S(1)}, u32[]{:S(2)}, u32[]{:S(2)}) %all-to-all-start.4) | async-done | bytes 131104 | tf_op jit(solution)/shard_map/all_to_all | solution.py:190
  171.7 4.6 all-to-all-start.6
  176.3 0.5 pad_maximum_fusion
  176.8 0.5 reshape.144
  177.5 0.9 copy.135
  178.4 13.0 %all-to-all-done.6 = bf16[8,64,128]{2,0,1:T(8,128)(2,1)S(1)} async-done(((bf16[8,64,128]{2,0,1:T(8,128)(2,1)}), bf16[8,64,128]{2,0,1:T(8,128)(2,1)S(1)}, u32[]{:S(2)}, u32[]{:S(2)}) %all-to-all-start.6) | async-done | bytes 131104 | tf_op jit(solution)/shard_map/all_to_all | solution.py:191
  191.4 4.6 all-to-all-start.8
  196.1 15.7 %all-to-all-done.8 = bf16[16,64,128]{2,0,1:T(8,128)(2,1)S(1)} async-done(((bf16[16,64,128]{2,0,1:T(8,128)(2,1)}), bf16[16,64,128]{2,0,1:T(8,128)(2,1)S(1)}, u32[]{:S(2)}, u32[]{:S(2)}) %all-to-all-start.8) | async-done | bytes 262176 | tf_op jit(solution)/shard_map/all_to_all | solution.py:195
  211.8 1.2 fusion.153
  213.0 0.4 fusion.151
  214.1 429.3 %all-reduce = (f32[64,33]{0,1:T(8,128)}, f32[64]{0:T(128)}, f32[64,64]{1,0:T(8,128)}, f32[64]{0:T(128)}) all-reduce(f32[64,33]{0,1:T(8,128)S(1)} %fusion.109, f32[64]{0:T(128)S(1)} %get-tuple-element.70, f32[64,64]{1,0:T(8,128)S(1)} %fusion.152, f32[64]{0:T(128)S(1)} %get-tuple-element.72), channel_id=1, replica_groups=mesh['dp'=8,'seq'=64] {'seq'}, use_global_device_ids=true, to_apply=%region_0.1 | all-reduce | flops 6336 | bytes 50688 | tf_op jit(solution)/shard_map/psum | solution.py:203
  643.4 5.2 reduce-scatter.2.cloned.1.call-done
  648.6 0.7 copy.185
  649.2 0.7 copy.186
  649.9 0.7 copy.187
  (87 shorter events, 10.4 us)
Async XLA Ops:
  7.2 39.2 %copy-start = (f32[1024,64]{0,1:T(8,128)S(1)}, f32[1024,64]{0,1:T(8,128)}, u32[]{:S(2)}) copy-start(f32[1024,64]{0,1:T(8,128)} %param.18) | copy-start | bytes 786436
  7.2 33.3 %all-to-all-start.1 = ((bf16[64,8,128]{2,1,0:T(8,128)(2,1)}), bf16[64,8,128]{2,1,0:T(8,128)(2,1)S(1)}, u32[]{:S(2)}, u32[]{:S(2)}) async-start(bf16[64,8,128]{2,1,0:T(8,128)(2,1)} %bitcast.181), calls=%async_computation.1 | async-start | bytes 262144 | tf_op jit(solution)/shard_map/all_to_all | solution.py:167
  26.3 14.2 %copy-start.21 = (f32[1,128]{1,0:T(1,128)}, f32[1,128]{1,0:T(1,128)S(1)}, u32[]{:S(2)}) copy-start(f32[1,128]{1,0:T(1,128)S(1)} %convert_multiply_fusion) | copy-start | bytes 1540
  28.1 0.6 copy-start.14
  30.3 30.3 %copy-start.16 = (f32[128,64]{0,1:T(8,128)}, f32[128,64]{0,1:T(8,128)S(1)}, u32[]{:S(2)}) copy-start(f32[128,64]{0,1:T(8,128)S(1)} %get-tuple-element.66) | copy-start | bytes 98308
  40.5 44.8 %copy-start.12 = (bf16[64,8,128]{2,1,0:T(8,128)(2,1)}, bf16[64,8,128]{2,1,0:T(8,128)(2,1)S(1)}, u32[]{:S(2)}) copy-start(bf16[64,8,128]{2,1,0:T(8,128)(2,1)S(1)} %all-to-all-done.1) | copy-start | bytes 393220
  40.5 20.1 %all-to-all-start.5 = ((bf16[64,8,128]{2,1,0:T(8,128)(2,1)}), bf16[64,8,128]{2,1,0:T(8,128)(2,1)S(1)}, u32[]{:S(2)}, u32[]{:S(2)}) async-start(bf16[64,8,128]{2,1,0:T(8,128)(2,1)} %bitcast.182), calls=%async_computation.5 | async-start | bytes 262144 | tf_op jit(solution)/shard_map/all_to_all | solution.py:139
  60.6 19.7 %all-to-all-start.2 = ((bf16[64,8,128]{2,1,0:T(8,128)(2,1)}), bf16[64,8,128]{2,1,0:T(8,128)(2,1)S(1)}, u32[]{:S(2)}, u32[]{:S(2)}) async-start(bf16[64,8,128]{2,1,0:T(8,128)(2,1)} %bitcast.183), calls=%async_computation.2 | async-start | bytes 262144 | tf_op jit(solution)/shard_map/all_to_all | solution.py:166
  65.5 41.4 %copy-start.4 = (f32[128,128]{0,1:T(8,128)}, f32[128,128]{0,1:T(8,128)S(1)}, u32[]{:S(2)}) copy-start(f32[128,128]{0,1:T(8,128)S(1)} %copy.95) | copy-start | bytes 196612
  65.6 41.3 %copy-start.7 = (f32[128,128]{0,1:T(8,128)}, f32[128,128]{0,1:T(8,128)S(1)}, u32[]{:S(2)}) copy-start(f32[128,128]{0,1:T(8,128)S(1)} %copy.96) | copy-start | bytes 196612
  80.3 20.5 %all-to-all-start = ((bf16[64,16,128]{2,1,0:T(8,128)(2,1)}), bf16[64,16,128]{2,1,0:T(8,128)(2,1)S(1)}, u32[]{:S(2)}, u32[]{:S(2)}) async-start(bf16[64,16,128]{2,1,0:T(8,128)(2,1)} %bitcast.4), calls=%async_computation | async-start | bytes 524288 | tf_op jit(solution)/shard_map/all_to_all | solution.py:150
  100.8 20.3 %all-to-all-start.3 = ((bf16[64,8,128]{2,1,0:T(8,128)(2,1)}), bf16[64,8,128]{2,1,0:T(8,128)(2,1)}, u32[]{:S(2)}, u32[]{:S(2)}) async-start(bf16[64,8,128]{2,1,0:T(8,128)(2,1)} %bitcast.21), calls=%async_computation.3 | async-start | bytes 262144 | tf_op jit(solution)/shard_map/all_to_all | solution.py:140
  107.9 1.0 copy-start.1
  107.9 1.3 copy-start.5
  107.9 1.3 copy-start.8
  121.1 1.4 copy-start.3
  123.7 1.0 copy-start.10
  124.1 2.9 copy-start.6
  124.1 2.9 copy-start.9
  125.6 1.9 copy-start.2
  129.5 0.9 copy-start.13
  130.1 27.3 %copy-start.11 = (bf16[8,64,128]{2,1,0:T(8,128)(2,1)S(1)}, bf16[8,64,128]{2,1,0:T(8,128)(2,1)}, u32[]{:S(2)}) copy-start(bf16[8,64,128]{2,1,0:T(8,128)(2,1)} %get-tuple-element.68) | copy-start | bytes 393220
  131.4 20.6 %all-to-all-start.7 = ((bf16[8,64,128]{2,0,1:T(8,128)(2,1)}), bf16[8,64,128]{2,0,1:T(8,128)(2,1)S(1)}, u32[]{:S(2)}, u32[]{:S(2)}) async-start(bf16[8,64,128]{2,0,1:T(8,128)(2,1)} %copy.126), calls=%async_computation.7 | async-start | bytes 262144 | tf_op jit(solution)/shard_map/all_to_all | solution.py:171
  152.1 19.7 %all-to-all-start.4 = ((bf16[8,64,128]{2,0,1:T(8,128)(2,1)}), bf16[8,64,128]{2,0,1:T(8,128)(2,1)S(1)}, u32[]{:S(2)}, u32[]{:S(2)}) async-start(bf16[8,64,128]{2,0,1:T(8,128)(2,1)} %copy.115), calls=%async_computation.4 | async-start | bytes 262144 | tf_op jit(solution)/shard_map/all_to_all | solution.py:190
  158.8 53.0 %copy-start.17 = (f32[128,64]{0,1:T(8,128)S(1)}, f32[128,64]{0,1:T(8,128)}, u32[]{:S(2)}) copy-start(f32[128,64]{0,1:T(8,128)} %copy-done.16) | copy-start | bytes 98308
  171.7 19.7 %all-to-all-start.6 = ((bf16[8,64,128]{2,0,1:T(8,128)(2,1)}), bf16[8,64,128]{2,0,1:T(8,128)(2,1)S(1)}, u32[]{:S(2)}, u32[]{:S(2)}) async-start(bf16[8,64,128]{2,0,1:T(8,128)(2,1)} %copy.121), calls=%async_computation.6 | async-start | bytes 262144 | tf_op jit(solution)/shard_map/all_to_all | solution.py:191
  176.8 36.1 %copy-start.19 = (f32[128,64]{0,1:T(8,128)S(1)}, f32[128,64]{0,1:T(8,128)}, u32[]{:S(2)}) copy-start(f32[128,64]{0,1:T(8,128)} %get-tuple-element.67) | copy-start | bytes 98308
  177.3 36.1 %copy-start.18 = (f32[64,64]{1,0:T(8,128)S(1)}, f32[64,64]{1,0:T(8,128)}, u32[]{:S(2)}) copy-start(f32[64,64]{1,0:T(8,128)} %param.16) | copy-start | bytes 49156
  177.3 36.1 %copy-start.20 = (f32[128,64]{0,1:T(8,128)S(1)}, f32[128,64]{0,1:T(8,128)}, u32[]{:S(2)}) copy-start(f32[128,64]{0,1:T(8,128)} %get-tuple-element.65) | copy-start | bytes 98308
  177.3 36.4 %copy-start.22 = (f32[1,128]{1,0:T(1,128)S(1)}, f32[1,128]{1,0:T(1,128)}, u32[]{:S(2)}) copy-start(f32[1,128]{1,0:T(1,128)} %copy-done.21) | copy-start | bytes 1540
  177.3 36.6 %copy-start.15 = (f32[128,64]{0,1:T(8,128)S(1)}, f32[128,64]{0,1:T(8,128)}, u32[]{:S(2)}) copy-start(f32[128,64]{0,1:T(8,128)} %copy-done.14) | copy-start | bytes 98308
  191.4 20.4 %all-to-all-start.8 = ((bf16[16,64,128]{2,0,1:T(8,128)(2,1)}), bf16[16,64,128]{2,0,1:T(8,128)(2,1)S(1)}, u32[]{:S(2)}, u32[]{:S(2)}) async-start(bf16[16,64,128]{2,0,1:T(8,128)(2,1)} %copy.135), calls=%async_computation.8 | async-start | bytes 524288 | tf_op jit(solution)/shard_map/all_to_all | solution.py:195
  196.0 452.6 %reduce-scatter.2.cloned.1.call-start = ((), (), s32[]{:S(2)}) async-start(), calls=%async_computation.10 | async-start | bytes 532480 | tf_op jit(solution)/shard_map/reduce_scatter | solution.py:198
Sparse Core Ops, SparseCore 0:
  213.1 435.4 reduce-scatter.1
where the time goes:
time: 658 us; the launch traced here: 657 us
  blocking collectives  429 us (65%)
  waiting for transfers between devices  122 us (19%)
  starting transfers between devices  57.7 us (9%)
  matrix products  18.1 us (3%)
  between operations  14.6 us (2%)
  local copies, waits for them, and re-layouts  8.39 us (1%)
  other arithmetic  7.39 us (1%)
    psum x1, blocking collectives, on_device(): lax.psum((partials[0], partials[1], partials[2], partials[3]), 'seq')  429 us
    all_to_all x1, starting transfers between devices, on_device(): lax.all_to_all(out_cotangent, 'seq', split_axis=0, concat_axis=1, tiled=T...  18.3 us
    all_to_all x1, waiting for transfers between devices, on_device(): lax.all_to_all(filter_grad_ch.astype(jnp.bfloat16), 'seq', split_axis=1,...  15.7 us
    all_to_all x1, waiting for transfers between devices, on_device(): lax.all_to_all(local_filters, 'seq', split_axis=0, concat_axis=1, tiled=T...  14.5 us
    all_to_all x1, waiting for transfers between devices, on_device(): lax.all_to_all(second_grad_ch, 'seq', split_axis=1, concat_axis=0, tiled=...  14 us
    all_to_all x1, waiting for transfers between devices, on_device(): lax.all_to_all(value_branch, 'seq', split_axis=0, concat_axis=1, tiled=True)  13.6 us
    all_to_all x1, waiting for transfers between devices, on_device(): lax.all_to_all(second_gate, 'seq', split_axis=0, concat_axis=1, tiled=True)  13.5 us
  transfers between devices with their start and end apart: 10, of which 10 were waited for; matrix products, arithmetic and copies ran while one was open for 3% of the time, Pallas kernels for 0%

commit v1 on v0

--- a/solution.py
+++ b/solution.py
@@ -163,7 +163,12 @@
         spectral_product(spec_two, spec_gated, False, False), tables, freq_rows, RADIX
     )
     second_ch, cot_ch = (
-        lax.all_to_all(second_gate, "seq", split_axis=0, concat_axis=1, tiled=True),
+        jnp.concatenate(
+            lax.all_to_all(
+                jnp.stack(jnp.split(second_gate, lax.axis_size("seq"), axis=0)), "seq", 0, 0
+            ),
+            axis=1,
+        ),
         lax.all_to_all(out_cotangent, "seq", split_axis=0, concat_axis=1, tiled=True),
     )
     cot_wide = cot_ch.astype(jnp.float32)

time: 658 us -> 741 us (1.13)
  local copies, waits for them, and re-layouts: 8.39 us -> 88.6 us
  starting transfers between devices: 57.7 us -> 67.8 us
  waiting for transfers between devices: 122 us -> 113 us
    unnamed x49 -> x112, local copies, waits for them, and re-layouts: 3.64 us -> 82.6 us
    all_to_all x1, waiting for transfers between devices: 10.2 us -> 0.01 us  [on_device(): lax.all_to_all(out_cotangent, 'seq', split_axis=0, concat_axis=1, tiled=T...]
    all_to_all x1, starting transfers between devices: 5.05 us -> 15.2 us  [on_device(): lax.all_to_all(value_branch, 'seq', split_axis=0, concat_axis=1, tiled=True)]
  transfers between devices with their start and end apart: 10 -> 10, of which waited for: 10 -> 9; matrix products, arithmetic and copies ran while one was open for 3% -> 14% of each run, Pallas kernels for 0% -> 0%
where the time goes in v1:
time: 741 us; the launch traced here: 738 us
  blocking collectives  429 us (58%)
  waiting for transfers between devices  113 us (15%)
  local copies, waits for them, and re-layouts  88.6 us (12%)
  starting transfers between devices  67.8 us (9%)
  matrix products  18.1 us (2%)
  between operations  14.7 us (2%)
  other arithmetic  7.43 us (1%)
    psum x1, blocking collectives, on_device(): lax.psum((partials[0], partials[1], partials[2], partials[3]), 'seq')  429 us
    unnamed x112, local copies, waits for them, and re-layouts  82.6 us
    all_to_all x1, starting transfers between devices, on_device(): lax.all_to_all(out_cotangent, 'seq', split_axis=0, concat_axis=1, tiled=T...  18.3 us
    all_to_all x1, waiting for transfers between devices, on_device(): lax.all_to_all(filter_grad_ch.astype(jnp.bfloat16), 'seq', split_axis=1,...  15.7 us
    all_to_all x1, starting transfers between devices, on_device(): lax.all_to_all(value_branch, 'seq', split_axis=0, concat_axis=1, tiled=True)  15.2 us
  transfers between devices with their start and end apart: 10, of which 9 were waited for; matrix products, arithmetic and copies ran while one was open for 14% of the time, Pallas kernels for 0%

profile of v1, /device:TPU:64, one launch (start us, length us, event | category | flops | bytes accessed | tf_op | source)
XLA Modules:
  0.0 738.4 jit_solution(5329434529734873287)
XLA Ops:
  7.2 18.3 %all-to-all-start.1 = ((bf16[64,8,128]{2,1,0:T(8,128)(2,1)}), bf16[64,8,128]{2,1,0:T(8,128)(2,1)S(1)}, u32[]{:S(2)}, u32[]{:S(2)}) async-start(bf16[64,8,128]{2,1,0:T(8,128)(2,1)} %bitcast.308), calls=%async_computation.1 | async-start | bytes 262144 | tf_op jit(solution)/shard_map/all_to_all | solution.py:172
  26.3 1.3 constant_dynamic-update-slice_fusion.63
  30.1 1.3 constant_dynamic-update-slice_fusion.60
  33.9 1.3 constant_dynamic-update-slice_fusion.57
  37.6 1.3 constant_dynamic-update-slice_fusion.54
  41.4 1.3 constant_dynamic-update-slice_fusion.51
  42.7 1.3 constant_dynamic-update-slice_fusion.50
  46.5 1.3 constant_dynamic-update-slice_fusion.47
  50.2 1.3 constant_dynamic-update-slice_fusion.44
  54.0 1.3 constant_dynamic-update-slice_fusion.41
  57.8 1.3 constant_dynamic-update-slice_fusion.38
  61.6 1.3 constant_dynamic-update-slice_fusion.35
  65.4 1.3 constant_dynamic-update-slice_fusion.32
  66.6 1.3 constant_dynamic-update-slice_fusion.31
  70.4 1.3 constant_dynamic-update-slice_fusion.28
  74.2 1.3 constant_dynamic-update-slice_fusion.25
  78.0 1.3 constant_dynamic-update-slice_fusion.22
  81.7 1.3 constant_dynamic-update-slice_fusion.19
  85.5 1.3 constant_dynamic-update-slice_fusion.16
  89.3 1.3 constant_dynamic-update-slice_fusion.13
  90.5 1.3 constant_dynamic-update-slice_fusion.12
  94.3 1.3 constant_dynamic-update-slice_fusion.9
  98.1 1.3 constant_dynamic-update-slice_fusion.6
  101.9 1.3 constant_dynamic-update-slice_fusion.3
  105.7 1.3 constant_dynamic-update-slice_fusion
  107.0 1.6 fusion.148
  109.0 1.6 fusion.149
  110.6 15.2 %all-to-all-start.5 = ((bf16[64,8,128]{2,1,0:T(8,128)(2,1)}), bf16[64,8,128]{2,1,0:T(8,128)(2,1)S(1)}, u32[]{:S(2)}, u32[]{:S(2)}) async-start(bf16[64,8,128]{2,1,0:T(8,128)(2,1)} %bitcast.309), calls=%async_computation.5 | async-start | bytes 262144 | tf_op jit(solution)/shard_map/all_to_all | solution.py:139
  127.3 13.6 %all-to-all-done.5 = bf16[64,8,128]{2,1,0:T(8,128)(2,1)S(1)} async-done(((bf16[64,8,128]{2,1,0:T(8,128)(2,1)}), bf16[64,8,128]{2,1,0:T(8,128)(2,1)S(1)}, u32[]{:S(2)}, u32[]{:S(2)}) %all-to-all-start.5) | async-done | bytes 131104 | tf_op jit(solution)/shard_map/all_to_all | solution.py:139
  140.9 4.6 all-to-all-start.2
  147.1 13.5 %all-to-all-done.2 = bf16[64,8,128]{2,1,0:T(8,128)(2,1)S(1)} async-done(((bf16[64,8,128]{2,1,0:T(8,128)(2,1)}), bf16[64,8,128]{2,1,0:T(8,128)(2,1)S(1)}, u32[]{:S(2)}, u32[]{:S(2)}) %all-to-all-start.2) | async-done | bytes 131104 | tf_op jit(solution)/shard_map/all_to_all | solution.py:167
  160.6 4.6 all-to-all-start
  166.6 14.5 %all-to-all-done = bf16[64,16,128]{2,1,0:T(8,128)(2,1)S(1)} async-done(((bf16[64,16,128]{2,1,0:T(8,128)(2,1)}), bf16[64,16,128]{2,1,0:T(8,128)(2,1)S(1)}, u32[]{:S(2)}, u32[]{:S(2)}) %all-to-all-start) | async-done | bytes 262176 | tf_op jit(solution)/shard_map/all_to_all | solution.py:150
  181.1 5.6 all-to-all-start.3
  190.7 1.3 fusion.17
  192.0 9.4 %all-to-all-done.3 = bf16[64,8,128]{2,1,0:T(8,128)(2,1)} async-done(((bf16[64,8,128]{2,1,0:T(8,128)(2,1)}), bf16[64,8,128]{2,1,0:T(8,128)(2,1)}, u32[]{:S(2)}, u32[]{:S(2)}) %all-to-all-start.3) | async-done | bytes 131104 | tf_op jit(solution)/shard_map/all_to_all | solution.py:140
  201.4 1.4 convolution_bitcast_fusion.1
  205.9 1.3 convolution_bitcast_fusion.3
  211.7 5.6 all-to-all-start.7
  218.4 14.0 %all-to-all-done.7 = bf16[8,64,128]{2,0,1:T(8,128)(2,1)S(1)} async-done(((bf16[8,64,128]{2,0,1:T(8,128)(2,1)}), bf16[8,64,128]{2,0,1:T(8,128)(2,1)S(1)}, u32[]{:S(2)}, u32[]{:S(2)}) %all-to-all-start.7) | async-done | bytes 131104 | tf_op jit(solution)/shard_map/all_to_all | solution.py:176
  232.3 4.6 all-to-all-start.4
  239.1 12.9 %all-to-all-done.4 = bf16[8,64,128]{2,0,1:T(8,128)(2,1)S(1)} async-done(((bf16[8,64,128]{2,0,1:T(8,128)(2,1)}), bf16[8,64,128]{2,0,1:T(8,128)(2,1)S(1)}, u32[]{:S(2)}, u32[]{:S(2)}) %all-to-all-start.4) | async-done | bytes 131104 | tf_op jit(solution)/shard_map/all_to_all | solution.py:195
  252.0 4.6 all-to-all-start.6
  258.7 13.0 %all-to-all-done.6 = bf16[8,64,128]{2,0,1:T(8,128)(2,1)S(1)} async-done(((bf16[8,64,128]{2,0,1:T(8,128)(2,1)}), bf16[8,64,128]{2,0,1:T(8,128)(2,1)S(1)}, u32[]{:S(2)}, u32[]{:S(2)}) %all-to-all-start.6) | async-done | bytes 131104 | tf_op jit(solution)/shard_map/all_to_all | solution.py:196
  271.6 4.6 all-to-all-start.8
  276.3 15.7 %all-to-all-done.8 = bf16[16,64,128]{2,0,1:T(8,128)(2,1)S(1)} async-done(((bf16[16,64,128]{2,0,1:T(8,128)(2,1)}), bf16[16,64,128]{2,0,1:T(8,128)(2,1)S(1)}, u32[]{:S(2)}, u32[]{:S(2)}) %all-to-all-start.8) | async-done | bytes 262176 | tf_op jit(solution)/shard_map/all_to_all | solution.py:200
  294.4 429.2 %all-reduce = (f32[64,33]{0,1:T(8,128)}, f32[64]{0:T(128)}, f32[64,64]{1,0:T(8,128)}, f32[64]{0:T(128)}) all-reduce(f32[64,33]{0,1:T(8,128)S(1)} %fusion.109, f32[64]{0:T(128)S(1)} %get-tuple-element.70, f32[64,64]{1,0:T(8,128)S(1)} %fusion.152, f32[64]{0:T(128)S(1)} %get-tuple-element.72), channel_id=1, replica_groups=mesh['dp'=8,'seq'=64] {'seq'}, use_global_device_ids=true, to_apply=%region_0.1 | all-reduce | flops 6336 | bytes 50688 | tf_op jit(solution)/shard_map/psum | solution.py:208
  723.6 6.0 reduce-scatter.2.cloned.1.call-done
  (151 shorter events, 76.7 us)
Async XLA Ops:
  7.2 119.5 %copy-start = (f32[1024,64]{0,1:T(8,128)S(1)}, f32[1024,64]{0,1:T(8,128)}, u32[]{:S(2)}) copy-start(f32[1024,64]{0,1:T(8,128)} %param.18) | copy-start | bytes 786436
  7.2 103.4 %all-to-all-start.1 = ((bf16[64,8,128]{2,1,0:T(8,128)(2,1)}), bf16[64,8,128]{2,1,0:T(8,128)(2,1)S(1)}, u32[]{:S(2)}, u32[]{:S(2)}) async-start(bf16[64,8,128]{2,1,0:T(8,128)(2,1)} %bitcast.308), calls=%async_computation.1 | async-start | bytes 262144 | tf_op jit(solution)/shard_map/all_to_all | solution.py:172
  26.3 82.7 %copy-start.21 = (f32[1,128]{1,0:T(1,128)}, f32[1,128]{1,0:T(1,128)S(1)}, u32[]{:S(2)}) copy-start(f32[1,128]{1,0:T(1,128)S(1)} %convert_multiply_fusion) | copy-start | bytes 1540
  108.7 51.9 %copy-start.14 = (f32[128,64]{0,1:T(8,128)}, f32[128,64]{0,1:T(8,128)S(1)}, u32[]{:S(2)}) copy-start(f32[128,64]{0,1:T(8,128)S(1)} %get-tuple-element.64) | copy-start | bytes 98308
  110.6 50.0 %copy-start.16 = (f32[128,64]{0,1:T(8,128)}, f32[128,64]{0,1:T(8,128)S(1)}, u32[]{:S(2)}) copy-start(f32[128,64]{0,1:T(8,128)S(1)} %get-tuple-element.66) | copy-start | bytes 98308
  110.6 55.0 %copy-start.12 = (bf16[64,8,128]{2,1,0:T(8,128)(2,1)}, bf16[64,8,128]{2,1,0:T(8,128)(2,1)S(1)}, u32[]{:S(2)}) copy-start(bf16[64,8,128]{2,1,0:T(8,128)(2,1)S(1)} %all-to-all-done.1) | copy-start | bytes 393220
  110.6 30.3 %all-to-all-start.5 = ((bf16[64,8,128]{2,1,0:T(8,128)(2,1)}), bf16[64,8,128]{2,1,0:T(8,128)(2,1)S(1)}, u32[]{:S(2)}, u32[]{:S(2)}) async-start(bf16[64,8,128]{2,1,0:T(8,128)(2,1)} %bitcast.309), calls=%async_computation.5 | async-start | bytes 262144 | tf_op jit(solution)/shard_map/all_to_all | solution.py:139
  140.9 19.7 %all-to-all-start.2 = ((bf16[64,8,128]{2,1,0:T(8,128)(2,1)}), bf16[64,8,128]{2,1,0:T(8,128)(2,1)S(1)}, u32[]{:S(2)}, u32[]{:S(2)}) async-start(bf16[64,8,128]{2,1,0:T(8,128)(2,1)} %constant_dynamic-update-slice_fusion), calls=%async_computation.2 | async-start | bytes 262144 | tf_op jit(solution)/shard_map/all_to_all | solution.py:167
  145.8 41.4 %copy-start.4 = (f32[128,128]{0,1:T(8,128)}, f32[128,128]{0,1:T(8,128)S(1)}, u32[]{:S(2)}) copy-start(f32[128,128]{0,1:T(8,128)S(1)} %copy.158) | copy-start | bytes 196612
  145.9 41.3 %copy-start.7 = (f32[128,128]{0,1:T(8,128)}, f32[128,128]{0,1:T(8,128)S(1)}, u32[]{:S(2)}) copy-start(f32[128,128]{0,1:T(8,128)S(1)} %copy.159) | copy-start | bytes 196612
  160.6 20.5 %all-to-all-start = ((bf16[64,16,128]{2,1,0:T(8,128)(2,1)}), bf16[64,16,128]{2,1,0:T(8,128)(2,1)S(1)}, u32[]{:S(2)}, u32[]{:S(2)}) async-start(bf16[64,16,128]{2,1,0:T(8,128)(2,1)} %bitcast.4), calls=%async_computation | async-start | bytes 524288 | tf_op jit(solution)/shard_map/all_to_all | solution.py:150
  181.1 20.3 %all-to-all-start.3 = ((bf16[64,8,128]{2,1,0:T(8,128)(2,1)}), bf16[64,8,128]{2,1,0:T(8,128)(2,1)}, u32[]{:S(2)}, u32[]{:S(2)}) async-start(bf16[64,8,128]{2,1,0:T(8,128)(2,1)} %bitcast.84), calls=%async_computation.3 | async-start | bytes 262144 | tf_op jit(solution)/shard_map/all_to_all | solution.py:140
  188.2 1.0 copy-start.1
  188.2 1.3 copy-start.5
  188.2 1.3 copy-start.8
  201.4 1.4 copy-start.3
  204.0 1.0 copy-start.10
  204.3 2.9 copy-start.6
  204.4 2.9 copy-start.9
  205.9 1.9 copy-start.2
  209.8 0.9 copy-start.13
  210.5 27.3 %copy-start.11 = (bf16[8,64,128]{2,1,0:T(8,128)(2,1)S(1)}, bf16[8,64,128]{2,1,0:T(8,128)(2,1)}, u32[]{:S(2)}) copy-start(bf16[8,64,128]{2,1,0:T(8,128)(2,1)} %get-tuple-element.68) | copy-start | bytes 393220
  211.7 20.6 %all-to-all-start.7 = ((bf16[8,64,128]{2,0,1:T(8,128)(2,1)}), bf16[8,64,128]{2,0,1:T(8,128)(2,1)S(1)}, u32[]{:S(2)}, u32[]{:S(2)}) async-start(bf16[8,64,128]{2,0,1:T(8,128)(2,1)} %copy.189), calls=%async_computation.7 | async-start | bytes 262144 | tf_op jit(solution)/shard_map/all_to_all | solution.py:176
  232.3 19.6 %all-to-all-start.4 = ((bf16[8,64,128]{2,0,1:T(8,128)(2,1)}), bf16[8,64,128]{2,0,1:T(8,128)(2,1)S(1)}, u32[]{:S(2)}, u32[]{:S(2)}) async-start(bf16[8,64,128]{2,0,1:T(8,128)(2,1)} %copy.178), calls=%async_computation.4 | async-start | bytes 262144 | tf_op jit(solution)/shard_map/all_to_all | solution.py:195
  239.0 53.0 %copy-start.17 = (f32[128,64]{0,1:T(8,128)S(1)}, f32[128,64]{0,1:T(8,128)}, u32[]{:S(2)}) copy-start(f32[128,64]{0,1:T(8,128)} %copy-done.16) | copy-start | bytes 98308
  252.0 19.6 %all-to-all-start.6 = ((bf16[8,64,128]{2,0,1:T(8,128)(2,1)}), bf16[8,64,128]{2,0,1:T(8,128)(2,1)S(1)}, u32[]{:S(2)}, u32[]{:S(2)}) async-start(bf16[8,64,128]{2,0,1:T(8,128)(2,1)} %copy.184), calls=%async_computation.6 | async-start | bytes 262144 | tf_op jit(solution)/shard_map/all_to_all | solution.py:196
  257.1 36.1 %copy-start.19 = (f32[128,64]{0,1:T(8,128)S(1)}, f32[128,64]{0,1:T(8,128)}, u32[]{:S(2)}) copy-start(f32[128,64]{0,1:T(8,128)} %get-tuple-element.67) | copy-start | bytes 98308
  257.6 36.1 %copy-start.18 = (f32[64,64]{1,0:T(8,128)S(1)}, f32[64,64]{1,0:T(8,128)}, u32[]{:S(2)}) copy-start(f32[64,64]{1,0:T(8,128)} %param.16) | copy-start | bytes 49156
  257.6 36.1 %copy-start.20 = (f32[128,64]{0,1:T(8,128)S(1)}, f32[128,64]{0,1:T(8,128)}, u32[]{:S(2)}) copy-start(f32[128,64]{0,1:T(8,128)} %get-tuple-element.65) | copy-start | bytes 98308
  257.6 36.4 %copy-start.22 = (f32[1,128]{1,0:T(1,128)S(1)}, f32[1,128]{1,0:T(1,128)}, u32[]{:S(2)}) copy-start(f32[1,128]{1,0:T(1,128)} %copy-done.21) | copy-start | bytes 1540
  257.6 36.6 %copy-start.15 = (f32[128,64]{0,1:T(8,128)S(1)}, f32[128,64]{0,1:T(8,128)}, u32[]{:S(2)}) copy-start(f32[128,64]{0,1:T(8,128)} %copy-done.14) | copy-start | bytes 98308
  271.6 20.4 %all-to-all-start.8 = ((bf16[16,64,128]{2,0,1:T(8,128)(2,1)}), bf16[16,64,128]{2,0,1:T(8,128)(2,1)S(1)}, u32[]{:S(2)}, u32[]{:S(2)}) async-start(bf16[16,64,128]{2,0,1:T(8,128)(2,1)} %copy.198), calls=%async_computation.8 | async-start | bytes 524288 | tf_op jit(solution)/shard_map/all_to_all | solution.py:200
  276.2 453.3 %reduce-scatter.2.cloned.1.call-start = ((), (), s32[]{:S(2)}) async-start(), calls=%async_computation.10 | async-start | bytes 532480 | tf_op jit(solution)/shard_map/reduce_scatter | solution.py:203
Sparse Core Ops, SparseCore 0:
  293.3 436.2 reduce-scatter.1
